TPU v7x, 32 devices: a whole 2x2x4 slice. The times are simulated.
32 devices in a mesh: rows: 8 (over z, y), vocab: 4 (over x, core).
Axes of the slice: x: 2, y: 2, z: 4, core: 2. Of those that a mesh axis runs over, the one named last changes fastest.
Arguments:
- hidden_policy: bfloat16 [512, 1536], P('rows', 'vocab'), may hold values from -45 to 45
- hidden_reference: bfloat16 [512, 1536], P('rows', 'vocab'), may hold values from -45 to 45
- gain_policy: bfloat16 [1536], replicated, may hold values from 0.5 to 1.5
- gain_reference: bfloat16 [1536], replicated, may hold values from 0.5 to 1.5
- head_policy: bfloat16 [1536, 16384], P(None, ('rows', 'vocab')), may hold values from -20 to 20
- head_reference: bfloat16 [1536, 16384], P(None, ('rows', 'vocab')), may hold values from -20 to 20
- targets: int32 [512], P('rows'), may hold values from 0 to 16383
- loss_mask: int32 [512], P('rows'), may hold values from 0 to 1, as said below
- doc_lengths: int32 [16], replicated, may hold values from 1 to 127, as said below
- doc_owner: int32 [16], replicated, may hold values from 0 to 7, as said below
- doc_score: float32 [16], replicated, may hold values from -3 to 6
Outputs:
- token_logprob: float32 [1024], P('rows')
- doc_advantage: float32 [16], P('rows')
Inputs may be any that keep to these rules, and one draw needn't show every extreme that they name: `loss_mask`: each index of rows holds at most 32 ones among its 64 tokens, and some index holds exactly 32. `doc_lengths`: documents lie end to end in the pack in this order; their lengths add up to 512. `doc_owner`: every index of rows owns exactly 2 documents, whose lengths add up to at most 128; for some index they add up to exactly 128.
All inputs are finite; a program needn't handle non-finite values.
Results may differ from a plain program's by a relative error of at most 0.0025.
Values may be sent and summed in bfloat16 or wider, within the bound.
A program may use at most 128 MiB of HBM per device.

v0:
```python
import jax
import jax.numpy as jnp
from jax import lax
from jax.sharding import PartitionSpec as P

DOC_DEV = 2
CAP = 128


epsilon = 1e-06
kl_weight = 0.1


def merged_2(part, axis, combine):
    gathered = jax.tree.map(lambda a: lax.all_gather(a, axis), part)

    def take(source):
        return jax.tree.map(lambda a: lax.dynamic_index_in_dim(a, source, 0, False), gathered)

    return lax.fori_loop(
        1, lax.axis_size(axis), lambda source, state: combine(state, take(source)), take(0)
    )


def final_norm(hidden, gain_vector):
    values = hidden.astype(jnp.float32)
    inverse_rms = lax.rsqrt(jnp.mean(values * values, axis=1, keepdims=True) + epsilon)
    return (values * inverse_rms * gain_vector.astype(jnp.float32)[None, :]).astype(jnp.bfloat16)


def column_stats(normed, head_shard, target_ids, column_base):
    logits = jnp.dot(normed, head_shard, preferred_element_type=jnp.float32)
    highest = jnp.max(logits, axis=1)
    exp_total = jnp.sum(jnp.exp(logits - highest[:, None]), axis=1)
    columns = jnp.arange(head_shard.shape[1], dtype=jnp.int32)[None, :] + column_base
    target_logit = jnp.sum(jnp.where(columns == target_ids[:, None], logits, 0.0), axis=1)
    return (highest, exp_total, target_logit)


def combine_stats(earlier, latter):
    merged = []
    for member in (0, 3):
        highest = jnp.maximum(earlier[member], latter[member])
        exp_total = earlier[member + 1] * jnp.exp(earlier[member] - highest) + latter[
            member + 1
        ] * jnp.exp(latter[member] - highest)
        merged.extend([highest, exp_total, earlier[member + 2] + latter[member + 2]])
    return tuple(merged)


def fold_sources(arrived):
    reduced = []
    for member in (0, 3):
        highest = jnp.max(arrived[member], axis=0)
        exp_total = jnp.sum(
            arrived[member + 1] * jnp.exp(arrived[member] - highest[None, :]), axis=0
        )
        reduced.extend([highest, exp_total, jnp.sum(arrived[member + 2], axis=0)])
    return tuple(reduced)


def doc_tables(doc_lengths, doc_owner):
    starts = jnp.cumsum(doc_lengths) - doc_lengths
    doc_order = jnp.arange(doc_lengths.shape[0], dtype=jnp.int32)
    before = (
        (doc_owner[None, :] == doc_owner[:, None]) & (doc_order[None, :] < doc_order[:, None])
    ).astype(jnp.int32)
    offset = jnp.sum(before * doc_lengths[None, :], axis=1)
    doc_rank = jnp.sum(before, axis=1)
    return (starts, offset, doc_rank)


def slot_table(owner_index, starts, offset, doc_rank, doc_lengths, doc_owner, slot_count):
    slot_index = jnp.arange(slot_count, dtype=jnp.int32)[:, None]
    inside = (
        (doc_owner[None, :] == owner_index)
        & (slot_index >= offset[None, :])
        & (slot_index < offset[None, :] + doc_lengths[None, :])
    ).astype(jnp.int32)
    slot_token = jnp.sum(inside * (starts[None, :] + slot_index - offset[None, :]), axis=1)
    slot_filled = jnp.sum(inside, axis=1)
    slot_doc = jnp.sum(inside * doc_rank[None, :], axis=1)
    return (slot_token, slot_filled, slot_doc)


def document_rewards(
    policy_lp,
    reference_lp,
    slot_mask,
    slot_doc,
    owner_index,
    doc_owner,
    doc_rank,
    doc_score,
    doc_slots,
):
    weights_mask = slot_mask.astype(jnp.float32)
    log_ratio = policy_lp - reference_lp
    kl_term = 0.5 * log_ratio * log_ratio
    doc_number = jnp.arange(doc_slots, dtype=jnp.int32)[:, None]
    doc_pick = (slot_doc[None, :] == doc_number).astype(jnp.float32)
    counts = jnp.sum(doc_pick * weights_mask[None, :], axis=1)
    kl_sum = jnp.sum(doc_pick * (weights_mask * kl_term)[None, :], axis=1)
    chosen = ((doc_owner[None, :] == owner_index) & (doc_rank[None, :] == doc_number)).astype(
        jnp.float32
    )
    doc_value = jnp.sum(chosen * doc_score[None, :], axis=1)
    reward = doc_value - kl_weight * kl_sum / jnp.maximum(counts, 1.0)
    return (reward, counts)


def per_device(
    hidden_policy,
    hidden_reference,
    gain_policy,
    gain_reference,
    head_policy,
    head_reference,
    targets,
    loss_mask,
    doc_lengths,
    doc_owner,
    doc_score,
):
    row_devices = lax.axis_size("rows")
    tok_dev = targets.shape[0]
    features = (
        lax.all_gather(hidden_policy, "vocab", axis=1, tiled=True),
        lax.all_gather(hidden_reference, "vocab", axis=1, tiled=True),
    )
    normed_policy = final_norm(features[0], gain_policy)
    normed_reference = final_norm(features[1], gain_reference)
    all_targets, all_mask = (
        lax.all_gather(targets, "rows", axis=0, tiled=True),
        lax.all_gather(loss_mask, "rows", axis=0, tiled=True),
    )
    column_base = lax.axis_index(("rows", "vocab")) * head_policy.shape[1]
    piece_stats = column_stats(
        lax.all_gather(normed_policy, "rows", axis=0, tiled=True),
        head_policy,
        all_targets,
        column_base,
    ) + column_stats(
        lax.all_gather(normed_reference, "rows", axis=0, tiled=True),
        head_reference,
        all_targets,
        column_base,
    )
    statistics = tuple((update for update in piece_stats))
    stat_index = jnp.arange(row_devices * tok_dev, dtype=jnp.int32)
    starts, offset, doc_rank = doc_tables(doc_lengths, doc_owner)
    owner_index = lax.axis_index("rows")
    every_owner = jnp.arange(row_devices, dtype=jnp.int32)
    tables = jax.vmap(
        lambda owner_value: slot_table(
            owner_value, starts, offset, doc_rank, doc_lengths, doc_owner, CAP
        )
    )(every_owner)
    owner_laid = tuple((jnp.take(values, jnp.take(stat_index, tables[0])) for values in statistics))
    arrived = lax.all_to_all(owner_laid, "rows", split_axis=0, concat_axis=0, tiled=True)
    own_stats = merged_2(fold_sources(arrived), "vocab", combine_stats)
    slot_token, slot_filled, slot_doc = tuple((table[owner_index] for table in tables))
    policy_lp = own_stats[2] - (own_stats[0] + jnp.log(own_stats[1]))
    reference_lp = own_stats[5] - (own_stats[3] + jnp.log(own_stats[4]))
    slot_mask = jnp.take(all_mask, slot_token) * slot_filled
    token_logprob = jnp.where(slot_mask == 1, policy_lp, 0.0)
    reward, counts = document_rewards(
        policy_lp,
        reference_lp,
        slot_mask,
        slot_doc,
        owner_index,
        doc_owner,
        doc_rank,
        doc_score,
        DOC_DEV,
    )
    weighted, token_total = lax.psum((jnp.sum(counts * reward), jnp.sum(counts)), "rows")
    return (token_logprob, reward - weighted / token_total)


def solution(mesh):
    return jax.shard_map(
        per_device,
        mesh=mesh,
        in_specs=(
            P("rows", "vocab"),
            P("rows", "vocab"),
            P(),
            P(),
            P(None, ("rows", "vocab")),
            P(None, ("rows", "vocab")),
            P("rows"),
            P("rows"),
            P(),
            P(),
            P(),
        ),
        out_specs=(P("rows"), P("rows")),
        check_vma=False,
    )
```

profile of v0, /device:TPU:0, one launch (start us, length us, event | category | flops | bytes accessed | tf_op | source)
XLA Modules:
  0.0 248.5 jit_solution(12319093220060869671)
XLA Ops:
  7.3 7.2 %all_gather.64 = bf16[64,1536]{1,0:T(8,128)(2,1)S(1)} all-gather(bf16[64,384]{1,0:T(8,128)(2,1)} %param.18), channel_id=1, replica_groups=mesh['rows'=8,'vocab'=4] {'vocab'}, dimensions={1}, use_global_device_ids=true | all-gather | bytes 245760 | tf_op jit(solution)/shard_map/all_gather | solution.py:129
  14.5 0.7 convert_element_type.37
  15.3 0.8 fusion.21
  16.2 0.7 convert_element_type.34
  16.9 5.8 %all_gather.55 = bf16[64,1536]{1,0:T(8,128)(2,1)S(1)} all-gather(bf16[64,384]{1,0:T(8,128)(2,1)} %param.17), channel_id=1, replica_groups=mesh['rows'=8,'vocab'=4] {'vocab'}, dimensions={1}, use_global_device_ids=true | all-gather | bytes 245760 | tf_op jit(solution)/shard_map/all_gather | solution.py:128
  22.8 0.8 fusion.18
  24.0 0.6 dynamic-slice
  25.2 0.2 dynamic-update-slice
  25.5 0.2 dynamic-update-slice.1
  26.2 6.9 %gather_fusion.1 = s32[1024]{0:T(1024)S(1)} fusion(s32[512]{0:T(512)S(1)} %iota.44, s32[1024]{0:T(1024)S(1)} %bitcast_clamp_fusion.1), kind=kCustom, calls=%fused_computation.clone | custom fusion | bytes 12288 | tf_op jit(solution)/shard_map/jit(_take)/gather | solution.py:159
  33.1 11.8 %all-reduce.2 = (s32[512]{0:T(512)S(1)}, s32[512]{0:T(512)S(1)}) all-reduce(s32[512]{0:T(512)S(1)} %dynamic-update-slice, s32[512]{0:T(512)S(1)} %dynamic-update-slice.1), channel_id=1, replica_groups=mesh['rows'=8,'vocab'=4] {'rows'}, use_global_device_ids=true, to_apply=%add | all-reduce | flops 1024 | bytes 8192
  45.0 1.3 gather_fusion
  46.3 15.7 %all-gather.17.cloned.1.call-done = bf16[512,1536]{1,0:T(8,128)(2,1)} async-done(((bf16[64,1536]{1,0:T(8,128)(2,1)}), bf16[512,1536]{1,0:T(8,128)(2,1)}) %all-gather.17.cloned.1.call-update) | async-done | bytes 1572880 | tf_op jit(solution)/shard_map/all_gather | solution.py:144
  62.0 2.4 fusion.33
  64.5 6.9 %gather_fusion.5 = f32[1024]{0:T(1024)S(1)} fusion(f32[512]{0:T(512)S(1)} %get-tuple-element.386, s32[1024]{0:T(1024)S(1)} %bitcast_clamp_fusion), kind=kCustom, calls=%fused_computation.4.clone | custom fusion | bytes 12288 | tf_op jit(solution)/shard_map/jit(_take)/gather | solution.py:159
  71.4 35.4 %all-gather.15.cloned.1.call-done = bf16[512,1536]{1,0:T(8,128)(2,1)} async-done(((bf16[64,1536]{1,0:T(8,128)(2,1)}), bf16[512,1536]{1,0:T(8,128)(2,1)}) %all-gather.15.cloned.1.call-update) | async-done | bytes 1572880 | tf_op jit(solution)/shard_map/all_gather | solution.py:139
  106.8 3.9 %fusion.34 = (f32[512]{0:T(512)S(1)}, f32[512,512]{0,1:T(8,128)}) fusion(bf16[512,1536]{1,0:T(8,128)(2,1)} %all-gather.15.cloned.1.call-done, bf16[1536,512]{1,0:T(8,128)(2,1)} %param.21), kind=kOutput, calls=%fused_computation.109 | convolution fusion | flops 805568000 | bytes 4196352 | tf_op jit(solution)/shard_map/dot_general | solution.py:32
  110.7 6.8 %gather_fusion.2 = f32[1024]{0:T(1024)S(1)} fusion(f32[512]{0:T(512)S(1)} %get-tuple-element.388, s32[1024]{0:T(1024)S(1)} %bitcast_clamp_fusion), kind=kCustom, calls=%fused_computation.1.clone | custom fusion | bytes 12288 | tf_op jit(solution)/shard_map/jit(_take)/gather | solution.py:159
  117.5 1.7 fusion.15
  119.3 6.9 %gather_fusion.7 = f32[1024]{0:T(1024)S(1)} fusion(f32[512]{0:T(512)S(1)} %get-tuple-element.323, s32[1024]{0:T(1024)S(1)} %bitcast_clamp_fusion), kind=kCustom, calls=%fused_computation.6.clone | custom fusion | bytes 12288 | tf_op jit(solution)/shard_map/jit(_take)/gather | solution.py:159
  126.1 0.6 bitcast_select_fusion
  126.7 6.8 %gather_fusion.6 = f32[1024]{0:T(1024)S(1)} fusion(f32[512]{0:T(512)S(1)} %get-tuple-element.324, s32[1024]{0:T(1024)S(1)} %bitcast_clamp_fusion), kind=kCustom, calls=%fused_computation.5.clone | custom fusion | bytes 12288 | tf_op jit(solution)/shard_map/jit(_take)/gather | solution.py:159
  133.6 6.9 %gather_fusion.4 = f32[1024]{0:T(1024)S(1)} fusion(f32[512]{0:T(512)S(1)} %get-tuple-element.331, s32[1024]{0:T(1024)S(1)} %bitcast_clamp_fusion), kind=kCustom, calls=%fused_computation.3.clone | custom fusion | bytes 12288 | tf_op jit(solution)/shard_map/jit(_take)/gather | solution.py:159
  140.5 6.9 %gather_fusion.3 = f32[1024]{0:T(1024)S(1)} fusion(f32[512]{0:T(512)S(1)} %get-tuple-element.330, s32[1024]{0:T(1024)S(1)} %bitcast_clamp_fusion), kind=kCustom, calls=%fused_computation.2.clone | custom fusion | bytes 12288 | tf_op jit(solution)/shard_map/jit(_take)/gather | solution.py:159
  147.3 0.6 bitcast_select_fusion.1
  148.0 3.3 %all-to-all-start = ((f32[8,1,128]{2,1,0:T(1,128)}), f32[8,1,128]{2,1,0:T(1,128)S(1)}, u32[]{:S(2)}, u32[]{:S(2)}) async-start(f32[8,1,128]{2,1,0:T(1,128)} %bitcast.17), calls=%async_computation | async-start | bytes 8192 | tf_op jit(solution)/shard_map/all_to_all | solution.py:160
  151.4 6.3 %all-to-all-done = f32[8,1,128]{2,1,0:T(1,128)S(1)} async-done(((f32[8,1,128]{2,1,0:T(1,128)}), f32[8,1,128]{2,1,0:T(1,128)S(1)}, u32[]{:S(2)}, u32[]{:S(2)}) %all-to-all-start) | async-done | bytes 4128 | tf_op jit(solution)/shard_map/all_to_all | solution.py:160
  157.7 3.3 %all-to-all-start.1 = ((f32[8,1,128]{2,1,0:T(1,128)}), f32[8,1,128]{2,1,0:T(1,128)S(1)}, u32[]{:S(2)}, u32[]{:S(2)}) async-start(f32[8,1,128]{2,1,0:T(1,128)} %bitcast.23), calls=%async_computation.1 | async-start | bytes 8192 | tf_op jit(solution)/shard_map/all_to_all | solution.py:160
  161.0 5.1 %all-gather.6 = f32[4,1,128]{2,1,0:T(1,128)S(1)} all-gather(f32[1,1,128]{2,1,0:T(1,128)S(1)} %bitcast.150), channel_id=2, replica_groups=mesh['rows'=8,'vocab'=4] {'vocab'}, dimensions={0}, use_global_device_ids=true | all-gather | bytes 2560 | tf_op jit(solution)/shard_map/all_gather | solution.py:15
  166.0 1.3 all-to-all-done.1
  167.4 4.6 %all-to-all-start.2 = ((f32[8,1,128]{2,1,0:T(1,128)}), f32[8,1,128]{2,1,0:T(1,128)S(1)}, u32[]{:S(2)}, u32[]{:S(2)}) async-start(f32[8,1,128]{2,1,0:T(1,128)} %bitcast.31), calls=%async_computation.2 | async-start | bytes 8192 | tf_op jit(solution)/shard_map/all_to_all | solution.py:160
  172.0 5.1 %all-gather.7 = f32[4,1,128]{2,1,0:T(1,128)S(1)} all-gather(f32[1,1,128]{2,1,0:T(1,128)S(1)} %bitcast.151), channel_id=3, replica_groups=mesh['rows'=8,'vocab'=4] {'vocab'}, dimensions={0}, use_global_device_ids=true | all-gather | bytes 2560 | tf_op jit(solution)/shard_map/all_gather | solution.py:15
  177.0 1.4 all-to-all-done.2
  178.5 4.6 %all-to-all-start.3 = ((f32[8,1,128]{2,1,0:T(1,128)}), f32[8,1,128]{2,1,0:T(1,128)S(1)}, u32[]{:S(2)}, u32[]{:S(2)}) async-start(f32[8,1,128]{2,1,0:T(1,128)} %bitcast.37), calls=%async_computation.3 | async-start | bytes 8192 | tf_op jit(solution)/shard_map/all_to_all | solution.py:160
  183.1 5.1 %all-gather.8 = f32[4,1,128]{2,1,0:T(1,128)S(1)} all-gather(f32[1,1,128]{2,1,0:T(1,128)S(1)} %bitcast.154), channel_id=4, replica_groups=mesh['rows'=8,'vocab'=4] {'vocab'}, dimensions={0}, use_global_device_ids=true | all-gather | bytes 2560 | tf_op jit(solution)/shard_map/all_gather | solution.py:15
  188.1 1.4 all-to-all-done.3
  189.5 4.6 %all-to-all-start.4 = ((f32[8,1,128]{2,1,0:T(1,128)}), f32[8,1,128]{2,1,0:T(1,128)S(1)}, u32[]{:S(2)}, u32[]{:S(2)}) async-start(f32[8,1,128]{2,1,0:T(1,128)} %bitcast.43), calls=%async_computation.4 | async-start | bytes 8192 | tf_op jit(solution)/shard_map/all_to_all | solution.py:160
  194.2 5.1 %all-gather.9 = f32[4,1,128]{2,1,0:T(1,128)S(1)} all-gather(f32[1,1,128]{2,1,0:T(1,128)S(1)} %bitcast.149), channel_id=5, replica_groups=mesh['rows'=8,'vocab'=4] {'vocab'}, dimensions={0}, use_global_device_ids=true | all-gather | bytes 2560 | tf_op jit(solution)/shard_map/all_gather | solution.py:15
  199.2 1.4 all-to-all-done.4
  200.6 4.6 %all-to-all-start.5 = ((f32[8,1,128]{2,1,0:T(1,128)}), f32[8,1,128]{2,1,0:T(1,128)S(1)}, u32[]{:S(2)}, u32[]{:S(2)}) async-start(f32[8,1,128]{2,1,0:T(1,128)} %bitcast.51), calls=%async_computation.5 | async-start | bytes 8192 | tf_op jit(solution)/shard_map/all_to_all | solution.py:160
  205.2 5.1 %all-gather.10 = f32[4,1,128]{2,1,0:T(1,128)S(1)} all-gather(f32[1,1,128]{2,1,0:T(1,128)S(1)} %bitcast.152), channel_id=6, replica_groups=mesh['rows'=8,'vocab'=4] {'vocab'}, dimensions={0}, use_global_device_ids=true | all-gather | bytes 2560 | tf_op jit(solution)/shard_map/all_gather | solution.py:15
  210.3 1.4 all-to-all-done.5
  211.7 5.1 %all-gather.11 = f32[4,1,128]{2,1,0:T(1,128)S(1)} all-gather(f32[1,1,128]{2,1,0:T(1,128)S(1)} %bitcast.153), channel_id=7, replica_groups=mesh['rows'=8,'vocab'=4] {'vocab'}, dimensions={0}, use_global_device_ids=true | all-gather | bytes 2560 | tf_op jit(solution)/shard_map/all_gather | solution.py:15
  217.0 0.5 compare_select_fusion.7
  217.5 0.6 select_reduce_fusion.3
  218.1 0.7 multiply_reduce_fusion.2
  218.8 21.0 %all-reduce.3 = (f32[]{:T(128)}, f32[]{:T(128)}) all-reduce(f32[]{:T(128)} %get-tuple-element.371, f32[]{:T(128)} %get-tuple-element.332), channel_id=1, replica_groups=mesh['rows'=8,'vocab'=4] {'rows'}, use_global_device_ids=true, to_apply=%region_26.29 | all-reduce | flops 2 | bytes 16 | tf_op jit(solution)/shard_map/psum | solution.py:178
  241.1 0.5 broadcast_subtract_fusion
  (63 shorter events, 1.9 us)
Async XLA Ops:
  7.2 54.9 %copy-start = (bf16[1536,512]{1,0:T(8,128)(2,1)S(1)}, bf16[1536,512]{1,0:T(8,128)(2,1)}, u32[]{:S(2)}) copy-start(bf16[1536,512]{1,0:T(8,128)(2,1)} %param.22) | copy-start | bytes 4718596
  7.2 16.8 %copy-start.6 = (u32[32]{0:T(128)S(1)}, u32[32]{0:T(128)}, u32[]{:S(2)}) copy-start(u32[32]{0:T(128)} %constant.141) | copy-start | bytes 388
  7.2 16.5 %copy-start.2 = (s32[16]{0:T(128)S(1)}, s32[16]{0:T(128)}, u32[]{:S(2)}) copy-start(s32[16]{0:T(128)} %param.26) | copy-start | bytes 196
  7.2 16.5 %copy-start.1 = (s32[16]{0:T(128)S(1)}, s32[16]{0:T(128)}, u32[]{:S(2)}) copy-start(s32[16]{0:T(128)} %param.25) | copy-start | bytes 196
  7.2 18.0 %copy-start.4 = (s32[64]{0:T(128)S(1)}, s32[64]{0:T(128)}, u32[]{:S(2)}) copy-start(s32[64]{0:T(128)} %param.24) | copy-start | bytes 772
  7.2 18.2 %copy-start.5 = (s32[64]{0:T(128)S(1)}, s32[64]{0:T(128)}, u32[]{:S(2)}) copy-start(s32[64]{0:T(128)} %param.23) | copy-start | bytes 772
  7.2 54.8 %all-gather.17.cloned.1.call-start = ((), (), s32[]{:S(2)}) async-start(), calls=%async_computation.7 | async-start | bytes 1769472 | tf_op jit(solution)/shard_map/all_gather | solution.py:144
  16.2 90.6 %all-gather.15.cloned.1.call-start = ((), (), s32[]{:S(2)}) async-start(), calls=%async_computation.6 | async-start | bytes 1769472 | tf_op jit(solution)/shard_map/all_gather | solution.py:139
  140.5 10.8 %copy-start.3 = (f32[16]{0:T(128)S(1)}, f32[16]{0:T(128)}, u32[]{:S(2)}) copy-start(f32[16]{0:T(128)} %param.27) | copy-start | bytes 196
  148.0 9.7 %all-to-all-start = ((f32[8,1,128]{2,1,0:T(1,128)}), f32[8,1,128]{2,1,0:T(1,128)S(1)}, u32[]{:S(2)}, u32[]{:S(2)}) async-start(f32[8,1,128]{2,1,0:T(1,128)} %bitcast.17), calls=%async_computation | async-start | bytes 8192 | tf_op jit(solution)/shard_map/all_to_all | solution.py:160
  157.7 9.7 %all-to-all-start.1 = ((f32[8,1,128]{2,1,0:T(1,128)}), f32[8,1,128]{2,1,0:T(1,128)S(1)}, u32[]{:S(2)}, u32[]{:S(2)}) async-start(f32[8,1,128]{2,1,0:T(1,128)} %bitcast.23), calls=%async_computation.1 | async-start | bytes 8192 | tf_op jit(solution)/shard_map/all_to_all | solution.py:160
  167.4 11.1 %all-to-all-start.2 = ((f32[8,1,128]{2,1,0:T(1,128)}), f32[8,1,128]{2,1,0:T(1,128)S(1)}, u32[]{:S(2)}, u32[]{:S(2)}) async-start(f32[8,1,128]{2,1,0:T(1,128)} %bitcast.31), calls=%async_computation.2 | async-start | bytes 8192 | tf_op jit(solution)/shard_map/all_to_all | solution.py:160
  178.5 11.1 %all-to-all-start.3 = ((f32[8,1,128]{2,1,0:T(1,128)}), f32[8,1,128]{2,1,0:T(1,128)S(1)}, u32[]{:S(2)}, u32[]{:S(2)}) async-start(f32[8,1,128]{2,1,0:T(1,128)} %bitcast.37), calls=%async_computation.3 | async-start | bytes 8192 | tf_op jit(solution)/shard_map/all_to_all | solution.py:160
  189.5 11.1 %all-to-all-start.4 = ((f32[8,1,128]{2,1,0:T(1,128)}), f32[8,1,128]{2,1,0:T(1,128)S(1)}, u32[]{:S(2)}, u32[]{:S(2)}) async-start(f32[8,1,128]{2,1,0:T(1,128)} %bitcast.43), calls=%async_computation.4 | async-start | bytes 8192 | tf_op jit(solution)/shard_map/all_to_all | solution.py:160
  200.6 11.1 %all-to-all-start.5 = ((f32[8,1,128]{2,1,0:T(1,128)}), f32[8,1,128]{2,1,0:T(1,128)S(1)}, u32[]{:S(2)}, u32[]{:S(2)}) async-start(f32[8,1,128]{2,1,0:T(1,128)} %bitcast.51), calls=%async_computation.5 | async-start | bytes 8192 | tf_op jit(solution)/shard_map/all_to_all | solution.py:160
Sparse Core Ops, SparseCore 0:
  16.3 45.7 all-gather.16
  64.2 42.5 all-gather.14
where the time goes:
time: 249 us; the launch traced here: 248 us
  blocking collectives  76.2 us (31%)
  waiting for transfers between devices  64.5 us (26%)
  local copies, waits for them, and re-layouts  50.4 us (20%)
  starting transfers between devices  25 us (10%)
  between operations  16.2 us (7%)
  other arithmetic  9.76 us (4%)
  matrix products  6.31 us (3%)
    gather x6, local copies, waits for them, and re-layouts, per_device(): jnp.take(values, jnp.take(stat_index, tables[0]))  41.1 us
    all_gather x1, waiting for transfers between devices, per_device(): lax.all_gather(normed_policy, 'rows', axis=0, tiled=True)  35.4 us
    all_gather x6, blocking collectives, merged_2(): gathered = jax.tree.map(lambda a: lax.all_gather(a, axis), part)  30.3 us
    all_to_all x6, starting transfers between devices, per_device(): lax.all_to_all(owner_laid, 'rows', split_axis=0, concat_axis=0, tiled=True)  24.9 us
    psum x1, blocking collectives, per_device(): lax.psum((jnp.sum(counts * reward), jnp.sum(counts)), 'rows')  21 us
    all_gather x1, waiting for transfers between devices, per_device(): lax.all_gather(normed_reference, 'rows', axis=0, tiled=True)  15.7 us
    all_to_all x6, waiting for transfers between devices, per_device(): lax.all_to_all(owner_laid, 'rows', split_axis=0, concat_axis=0, tiled=True)  13.3 us
    unnamed x1, blocking collectives  11.8 us
  transfers between devices with their start and end apart: 8, of which 8 were waited for; matrix products, arithmetic and copies ran while one was open for 9% of the time, Pallas kernels for 0%

commit v1 on v0

v1 whole, which is shorter than its diff:
```python
import functools

import jax
import jax.numpy as jnp
from jax import lax
from jax.experimental import pallas as pl
from jax.experimental.pallas import tpu as pltpu
from jax.sharding import PartitionSpec as P

DOC_DEV = 2
CAP = 128
RESP_DEV = 32

epsilon = 1e-06
kl_weight = 0.1
MESH = pl.DeviceIdType.MESH
F32 = jnp.float32
BF16 = jnp.bfloat16
LANES = 128


def iota(shape, dim):
    return lax.broadcasted_iota(jnp.int32, shape, dim)


def row_to_col(row):
    n = row.shape[1]
    return jnp.sum(jnp.where(iota((n, n), 0) == iota((n, n), 1), row, 0.0), axis=1, keepdims=True)


def col_to_row(col):
    n = col.shape[0]
    return jnp.sum(jnp.where(iota((n, n), 0) == iota((n, n), 1), col, 0.0), axis=0, keepdims=True)


def kernel(
    rows,
    vocab,
    hidden_p,
    hidden_r,
    gain_p,
    gain_r,
    head_p,
    head_r,
    targets,
    mask,
    lengths,
    owners,
    scores,
    out_lp,
    out_adv,
    heads,
    gathered,
    meta,
    stats,
    head_sem,
    send_sem,
    recv_sem,
    core_send,
    core_recv,
    meta_send,
    meta_recv,
    stat_send,
    stat_recv,
):
    Y, C = 2, 2
    Z, X = rows // Y, vocab // C
    tok, feat = hidden_p.shape
    resp = gathered.shape[4]
    n_tok = rows * resp
    vcols = heads.shape[2]
    r, v = lax.axis_index("rows"), lax.axis_index("vocab")
    z, y = r // Y, r % Y
    x, c = v // C, v % C
    devices = rows * vocab
    me = r * vocab + v

    head_copies = [
        pltpu.make_async_copy(src, heads.at[i], head_sem.at[i])
        for i, src in enumerate((head_p, head_r))
    ]
    for copy in head_copies:
        copy.start()

    barrier = pltpu.get_barrier_semaphore()
    for step in range(1, devices):
        other = (me + step) % devices
        pl.semaphore_signal(
            barrier, inc=1, device_id=(other // vocab, other % vocab), device_id_type=MESH
        )

    tri = (iota((tok, tok), 0) <= iota((tok, tok), 1)).astype(F32)

    def pick_of(mask_row):
        running = jnp.dot(
            jnp.broadcast_to(mask_row, (8, tok)).astype(BF16),
            tri.astype(BF16),
            preferred_element_type=F32,
        )[0:1]
        slots = iota((resp, tok), 0).astype(F32)
        return ((running - 1.0) == slots) & (mask_row == 1.0)

    own_mask = mask[...].astype(F32)
    own_pick = pick_of(own_mask).astype(BF16)
    for m, hidden in enumerate((hidden_p, hidden_r)):
        gathered[m, v, y, z] = jnp.dot(
            own_pick, hidden[...], preferred_element_type=F32
        ).astype(BF16)
    own_meta = y * Z + z
    meta[own_meta, 0:1, 0:tok] = targets[...]
    meta[own_meta, 1:2, 0:tok] = mask[...]
    pl.semaphore_wait(barrier, devices - 1)

    sends = []

    def block(m, ay, ax, d, core):
        return gathered.at[m, ((x + X - ax) % X) * C + core, (y + Y - ay) % Y, (z + Z - d) % Z]

    def remote(src, dst, s_sem, r_sem, dev):
        return pltpu.make_async_remote_copy(
            src_ref=src, dst_ref=dst, send_sem=s_sem, recv_sem=r_sem, device_id=dev, device_id_type=MESH
        )

    def send(m, held, moved, dev):
        src = block(m, *held, c)
        copy = remote(src, src, send_sem.at[(m, *moved)], recv_sem.at[(m, *moved)], dev)
        copy.start()
        sends.append(copy)

    def arrived(m, at):
        dst = block(m, *at, c)
        remote(dst, dst, send_sem.at[(m, *at)], recv_sem.at[(m, *at)], (r, v)).wait_recv()

    def to_core(m, at):
        src = block(m, *at, c)
        copy = remote(src, src, core_send.at[(m, *at)], core_recv.at[(m, *at)], (r, x * C + 1 - c))
        copy.start()
        sends.append(copy)

    for d in range(1, Z):
        for m in (0, 1):
            send(m, (0, 0, 0), (0, 0, d), (((z + d) % Z) * Y + y, v))
    for step in range(1, rows):
        other = (r + step) % rows
        copy = remote(
            meta.at[own_meta], meta.at[own_meta], meta_send.at[step], meta_recv.at[step], (other, v)
        )
        copy.start()
        sends.append(copy)

    def along_y(m, ax, d):
        send(m, (0, ax, d), (1, ax, d), (z * Y + 1 - y, v))

    def along_x(m, ay, d):
        for dx in range(1, X):
            send(m, (ay, 0, d), (ay, dx, d), (r, ((x + dx) % X) * C + c))

    for d in range(Z):
        for m in (0, 1):
            if d:
                arrived(m, (0, 0, d))
            if m == 0:
                along_y(m, 0, d)
            else:
                along_x(m, 0, d)
            to_core(m, (0, 0, d))
    for d in range(Z):
        along_x(0, 0, d)
        along_y(1, 0, d)
        arrived(0, (1, 0, d))
        along_x(0, 1, d)
        to_core(0, (1, 0, d))
        for dx in range(1, X):
            arrived(1, (0, dx, d))
            along_y(1, dx, d)
            to_core(1, (0, dx, d))
    for d in range(Z):
        for dx in range(1, X):
            for ay in range(Y):
                arrived(0, (ay, dx, d))
                to_core(0, (ay, dx, d))
        for dx in range(X):
            arrived(1, (1, dx, d))
            to_core(1, (1, dx, d))

    for step in range(1, rows):
        src = (r + rows - step) % rows
        slot = (src % Y) * Z + src // Y
        remote(
            meta.at[slot], meta.at[slot], meta_send.at[step], meta_recv.at[step], (r, v)
        ).wait_recv()
    target_cols, pos_cols, flag_cols = [], [], []
    for q in range(rows):
        pack = (q % Z) * Y + q // Z
        row_mask = meta[q, 1:2, 0:tok].astype(F32)
        pick = pick_of(row_mask)
        row_targets = meta[q, 0:1, 0:tok].astype(F32)
        where_at = (iota((1, tok), 1) + pack * tok).astype(F32)
        target_cols.append(jnp.sum(jnp.where(pick, row_targets, 0.0), axis=1, keepdims=True))
        pos_cols.append(jnp.sum(jnp.where(pick, where_at, 0.0), axis=1, keepdims=True))
        flag_cols.append(jnp.sum(jnp.where(pick, 1.0, 0.0), axis=1, keepdims=True))
    target_col = jnp.concatenate(target_cols, axis=0)
    pos_col = jnp.concatenate(pos_cols, axis=0)
    flag_col = jnp.concatenate(flag_cols, axis=0)
    base = (me * vcols).astype(F32)
    hit = iota((n_tok, vcols), 1).astype(F32) == (target_col - base)

    stat_cols = []
    for m, gain in enumerate((gain_p, gain_r)):
        for d in range(Z):
            for ay in range(Y):
                for ax in range(X):
                    dst = block(m, ay, ax, d, 1 - c)
                    remote(
                        dst, dst, core_send.at[m, ay, ax, d], core_recv.at[m, ay, ax, d], (r, v)
                    ).wait_recv()
        head_copies[m].wait()
        total = jnp.zeros((n_tok, 1), F32)
        for part in range(vocab):
            piece = gathered[m, part].reshape(n_tok, feat).astype(F32)
            total = total + jnp.sum(piece * piece, axis=1, keepdims=True)
        inverse_rms = lax.rsqrt(total / (feat * vocab) + epsilon)
        logits = jnp.zeros((n_tok, vcols), F32)
        for part in range(vocab):
            piece = gathered[m, part].reshape(n_tok, feat).astype(F32)
            weight = gain[0:1, part * feat : (part + 1) * feat].astype(F32)
            normed = (piece * inverse_rms * weight).astype(BF16)
            logits = logits + jnp.dot(
                normed, heads[m, part * feat : (part + 1) * feat, :], preferred_element_type=F32
            )
        highest = jnp.max(logits, axis=1, keepdims=True)
        lse = highest + jnp.log(jnp.sum(jnp.exp(logits - highest), axis=1, keepdims=True))
        stat_cols += [lse, jnp.sum(jnp.where(hit, logits, 0.0), axis=1, keepdims=True)]

    lane = iota((n_tok, LANES), 1)
    packed = jnp.zeros((n_tok, LANES), F32)
    for i, col in enumerate(stat_cols + [pos_col, flag_col]):
        packed = jnp.where(lane == i, col, packed)
    turned = jnp.transpose(packed)
    stats[me] = turned[0:4]
    pos, flag = turned[4:5], turned[5:6]

    docs = lengths.shape[1]
    length_row = lengths[...].astype(F32)
    owner_row = owners[...].astype(F32)
    length_col, owner_col = row_to_col(length_row), row_to_col(owner_row)
    score_col = row_to_col(scores[...])
    earlier = iota((docs, docs), 1) < iota((docs, docs), 0)
    starts = jnp.sum(jnp.where(earlier, length_row, 0.0), axis=1, keepdims=True)
    before = earlier & (owner_col == owner_row)
    offset = jnp.sum(jnp.where(before, length_row, 0.0), axis=1, keepdims=True)
    rank = jnp.sum(jnp.where(before, 1.0, 0.0), axis=1, keepdims=True)
    inside = (pos >= starts) & (pos < starts + length_col) & (flag == 1.0)
    counts = jnp.sum(jnp.where(inside, 1.0, 0.0), axis=1, keepdims=True)
    mine = owner_col == r.astype(F32)
    slot = jnp.sum(
        jnp.where(inside & mine, offset + pos - starts + 1.0, 0.0), axis=0, keepdims=True
    )
    lands = iota((CAP, n_tok), 0).astype(F32) == slot - 1.0

    for step in range(1, devices):
        other = (me + step) % devices
        copy = remote(
            stats.at[me],
            stats.at[me],
            stat_send.at[step],
            stat_recv.at[step],
            (other // vocab, other % vocab),
        )
        copy.start()
        sends.append(copy)
    for step in range(1, devices):
        src = (me + devices - step) % devices
        remote(
            stats.at[src], stats.at[src], stat_send.at[step], stat_recv.at[step], (r, v)
        ).wait_recv()

    every = stats[...]
    top = jnp.max(every, axis=0)
    spread = jnp.log(jnp.sum(jnp.exp(every - top[None]), axis=0)) + top
    summed = jnp.sum(every, axis=0)
    lp_p = summed[1:2] - spread[0:1]
    lp_r = summed[3:4] - spread[2:3]
    ratio = lp_p - lp_r
    kl = 0.5 * ratio * ratio
    kl_sum = jnp.sum(jnp.where(inside, kl, 0.0), axis=1, keepdims=True)
    reward = score_col - kl_weight * kl_sum / jnp.maximum(counts, 1.0)
    baseline = jnp.sum(counts * reward, axis=0, keepdims=True) / jnp.sum(
        counts, axis=0, keepdims=True
    )
    advantage = reward - baseline
    lane_doc = iota((docs, LANES), 1).astype(F32)
    out_adv[...] = jnp.sum(
        jnp.where(mine & (rank == lane_doc), advantage, 0.0), axis=0, keepdims=True
    )
    out_lp[...] = col_to_row(jnp.sum(jnp.where(lands, lp_p, 0.0), axis=1, keepdims=True))
    for copy in sends:
        copy.wait_send()


def per_device(
    rows,
    vocab,
    hidden_policy,
    hidden_reference,
    gain_policy,
    gain_reference,
    head_policy,
    head_reference,
    targets,
    loss_mask,
    doc_lengths,
    doc_owner,
    doc_score,
):
    row = lambda a: a.reshape(1, a.shape[0])
    feat = hidden_policy.shape[1]
    width, vcols = head_policy.shape
    z, x = rows // 2, vocab // 2
    n_tok = rows * RESP_DEV
    devices = rows * vocab
    vmem = pl.BlockSpec(memory_space=pltpu.VMEM)
    hbm = pl.BlockSpec(memory_space=pl.ANY)
    dma = pltpu.SemaphoreType.DMA
    lp, adv = pl.pallas_call(
        functools.partial(kernel, rows, vocab),
        out_shape=(
            jax.ShapeDtypeStruct((1, CAP), F32),
            jax.ShapeDtypeStruct((1, LANES), F32),
        ),
        in_specs=[vmem] * 4 + [hbm] * 2 + [vmem] * 5,
        out_specs=(vmem, vmem),
        scratch_shapes=[
            pltpu.VMEM((2, width, vcols), BF16),
            pltpu.VMEM((2, vocab, 2, z, RESP_DEV, feat), BF16),
            pltpu.VMEM((rows, 2, LANES), jnp.int32),
            pltpu.VMEM((devices, 4, n_tok), F32),
            dma((2,)),
            dma((2, 2, x, z)),
            dma((2, 2, x, z)),
            dma((2, 2, x, z)),
            dma((2, 2, x, z)),
            dma((rows,)),
            dma((rows,)),
            dma((devices,)),
            dma((devices,)),
        ],
        compiler_params=pltpu.CompilerParams(
            collective_id=0, has_side_effects=True, vmem_limit_bytes=60 * 1024 * 1024
        ),
    )(
        hidden_policy,
        hidden_reference,
        row(gain_policy),
        row(gain_reference),
        head_policy,
        head_reference,
        row(targets),
        row(loss_mask),
        row(doc_lengths),
        row(doc_owner),
        row(doc_score),
    )
    return lp.reshape(CAP), adv[0, :DOC_DEV]


def solution(mesh):
    return jax.shard_map(
        functools.partial(per_device, mesh.shape["rows"], mesh.shape["vocab"]),
        mesh=mesh,
        in_specs=(
            P("rows", "vocab"),
            P("rows", "vocab"),
            P(),
            P(),
            P(None, ("rows", "vocab")),
            P(None, ("rows", "vocab")),
            P("rows"),
            P("rows"),
            P(),
            P(),
            P(),
        ),
        out_specs=(P("rows"), P("rows")),
        check_vma=False,
    )
```

time: 249 us -> 36.2 us (0.15)
  blocking collectives: 76.2 us -> 0 us
  waiting for transfers between devices: 64.5 us -> 0 us
  local copies, waits for them, and re-layouts: 50.4 us -> 4.88 us
  Pallas kernels: 0 us -> 30.4 us
  starting transfers between devices: 25 us -> 0 us
  between operations: 16.2 us -> 0.64 us
  other arithmetic: 9.76 us -> 0 us
  matrix products: 6.31 us -> 0 us
    all_gather x2 -> x0, waiting for transfers between devices: 51.2 us -> none  [the longest x1 35.4 us: per_device(): lax.all_gather(normed_policy, 'rows', axis=0, tiled=True)]
    gather x8 -> x0, local copies, waits for them, and re-layouts: 49.3 us -> none  [the longest x6 41.1 us: per_device(): jnp.take(values, jnp.take(stat_index, tables[0]))]
    all_gather x8 -> x0, blocking collectives: 43.3 us -> none  [the longest x6 30.3 us: merged_2(): gathered = jax.tree.map(lambda a: lax.all_gather(a, axis), part)]
    pallas_call x0 -> x1, Pallas kernels: none -> 30.4 us  [per_device(): pl.pallas_call(functools.partial(kernel, rows, vocab), out_shape=(jax.Sha...]
    all_to_all x6 -> x0, starting transfers between devices: 24.9 us -> none  [per_device(): lax.all_to_all(owner_laid, 'rows', split_axis=0, concat_axis=0, tiled=True)]
    psum x1 -> x0, blocking collectives: 21 us -> none  [per_device(): lax.psum((jnp.sum(counts * reward), jnp.sum(counts)), 'rows')]
    all_to_all x6 -> x0, waiting for transfers between devices: 13.3 us -> none  [per_device(): lax.all_to_all(owner_laid, 'rows', split_axis=0, concat_axis=0, tiled=True)]
    unnamed x1 -> x0, blocking collectives: 11.8 us -> none
  transfers between devices with their start and end apart: 8 -> 0, of which waited for: 8 -> 0; matrix products, arithmetic and copies ran while one was open for 9% -> 0% of each run, Pallas kernels for 0% -> 0%
where the time goes in v1:
time: 36.2 us; the launch traced here: 36 us
  Pallas kernels  30.4 us (84%)
  local copies, waits for them, and re-layouts  4.88 us (13%)
  between operations  0.64 us (2%)
    pallas_call x1, Pallas kernels, per_device(): pl.pallas_call(functools.partial(kernel, rows, vocab), out_shape=(jax.Sha...  30.4 us
    reshape x2, local copies, waits for them, and re-layouts, per_device(): row = lambda a: a.reshape(1, a.shape[0])  2.56 us
    unnamed x1, local copies, waits for them, and re-layouts  1.18 us
    squeeze x1, local copies, waits for them, and re-layouts, per_device(): return (lp.reshape(CAP), adv[0, :DOC_DEV])  1.15 us

profile of v1, /device:TPU:0, one launch (start us, length us, event | category | flops | bytes accessed | tf_op | source)
XLA Modules:
  0.0 36.0 jit_solution(15448428978230935871)
XLA Ops:
  0.6 1.3 %reshape.28.gain_p = bf16[1,1536]{1,0:T(2,128)(2,1)} reshape(bf16[1536]{0:T(1024)(128)(2,1)} %param.13) | data formatting | bytes 6144 | tf_op jit(solution)/shard_map/reshape | solution.py:316
  1.9 1.3 %reshape.29.gain_r = bf16[1,1536]{1,0:T(2,128)(2,1)} reshape(bf16[1536]{0:T(1024)(128)(2,1)} %param.14) | data formatting | bytes 6144 | tf_op jit(solution)/shard_map/reshape | solution.py:316
  3.2 30.4 %shard_map.122 = (f32[1,128]{1,0:T(1,128)}, f32[1,128]{1,0:T(1,128)}) custom-call(bf16[64,384]{1,0:T(8,128)(2,1)} %hidden_p.1, bf16[64,384]{1,0:T(8,128)(2,1)} %hidden_r.1, bf16[1,1536]{1,0:T(2,128)(2,1)} %reshape.28.gain_p, bf16[1,1536]{1,0:T(2,128)(2,1)} %reshape.29.gain_r, bf16[1536,512]{1,0:T(8,128)(2,1)} %head_p.1, bf16[1536,512]{1,0:T(8,128)(2,1)} %head_r.1, ...), custom_call_target="tpu_custom_call" | custom-call | tf_op jit(solution)/shard_map/pallas_call | solution.py:325
  33.6 1.1 %slice_bitcast_fusion = f32[2]{0:T(128)} fusion(f32[1,128]{1,0:T(1,128)} %get-tuple-element.5), kind=kLoop, calls=%fused_computation | loop fusion | bytes 16 | tf_op jit(solution)/shard_map/squeeze | solution.py:364
  34.8 1.2 %copy.14 = f32[128]{0:T(128)} copy(f32[128]{0:T(128)} %bitcast.13) | data formatting | bytes 1024

commit v2 on v1

--- a/solution.py
+++ b/solution.py
@@ -58,6 +58,7 @@
     recv_sem,
     core_send,
     core_recv,
+    line_send,
     meta_send,
     meta_recv,
     stat_send,
@@ -83,11 +84,16 @@
         copy.start()
 
     barrier = pltpu.get_barrier_semaphore()
-    for step in range(1, devices):
-        other = (me + step) % devices
-        pl.semaphore_signal(
-            barrier, inc=1, device_id=(other // vocab, other % vocab), device_id_type=MESH
-        )
+
+    def greet(dev):
+        pl.semaphore_signal(barrier, inc=1, device_id=dev, device_id_type=MESH)
+
+    greet((r, x * C + 1 - c))
+    greet((z * Y + 1 - y, v))
+    for dx in range(1, X):
+        greet((r, ((x + dx) % X) * C + c))
+    for step in range(1, Z):
+        greet((((z + step) % Z) * Y + y, v))
 
     tri = (iota((tok, tok), 0) <= iota((tok, tok), 1)).astype(F32)
 
@@ -109,86 +115,104 @@
     own_meta = y * Z + z
     meta[own_meta, 0:1, 0:tok] = targets[...]
     meta[own_meta, 1:2, 0:tok] = mask[...]
-    pl.semaphore_wait(barrier, devices - 1)
+    pl.semaphore_wait(barrier, X + Z)
 
     sends = []
 
-    def block(m, ay, ax, d, core):
-        return gathered.at[m, ((x + X - ax) % X) * C + core, (y + Y - ay) % Y, (z + Z - d) % Z]
+    near = jnp.minimum(z, Z - 1 - z)
+    order = [z]
+    for t in range(1, Z):
+        paired = z - (t + 1) // 2 if t % 2 else z + t // 2
+        beyond = jnp.where(z > Z - 1 - z, z - (t - near), z + (t - near))
+        order.append(jnp.where(t <= 2 * near, paired, beyond))
+
+    def block(m, ay, ax, zz, core):
+        return gathered.at[m, ((x + X - ax) % X) * C + core, (y + Y - ay) % Y, zz]
 
     def remote(src, dst, s_sem, r_sem, dev):
         return pltpu.make_async_remote_copy(
             src_ref=src, dst_ref=dst, send_sem=s_sem, recv_sem=r_sem, device_id=dev, device_id_type=MESH
         )
 
-    def send(m, held, moved, dev):
-        src = block(m, *held, c)
-        copy = remote(src, src, send_sem.at[(m, *moved)], recv_sem.at[(m, *moved)], dev)
+    def start(ref, s_sem, r_sem, dev):
+        copy = remote(ref, ref, s_sem, r_sem, dev)
         copy.start()
         sends.append(copy)
 
-    def arrived(m, at):
-        dst = block(m, *at, c)
-        remote(dst, dst, send_sem.at[(m, *at)], recv_sem.at[(m, *at)], (r, v)).wait_recv()
-
-    def to_core(m, at):
-        src = block(m, *at, c)
-        copy = remote(src, src, core_send.at[(m, *at)], core_recv.at[(m, *at)], (r, x * C + 1 - c))
-        copy.start()
-        sends.append(copy)
-
-    for d in range(1, Z):
+    def send(m, held, moved, zz, dev):
+        start(block(m, *held, zz, c), send_sem.at[(m, *moved, zz)], recv_sem.at[(m, *moved, zz)], dev)
+
+    def landed(ref, s_sem, r_sem):
+        remote(ref, ref, s_sem, r_sem, (r, v)).wait_recv()
+
+    def arrived(m, ay, ax, zz):
+        landed(block(m, ay, ax, zz, c), send_sem.at[m, ay, ax, zz], recv_sem.at[m, ay, ax, zz])
+
+    def to_core(m, ay, ax, zz):
+        start(
+            block(m, ay, ax, zz, c),
+            core_send.at[m, ay, ax, zz],
+            core_recv.at[m, ay, ax, zz],
+            (r, x * C + 1 - c),
+        )
+
+    def along_y(m, ax, zz):
+        send(m, (0, ax), (1, ax), zz, (z * Y + 1 - y, v))
+
+    def along_x(m, ay, zz):
+        for dx in range(1, X):
+            send(m, (ay, 0), (ay, dx), zz, (r, ((x + dx) % X) * C + c))
+
+    def meta_at(ay, zz):
+        return meta.at[((y + Y - ay) % Y) * Z + zz]
+
+    def pass_on(t, zz, part):
+        if t:
+            return
+        ref = meta_at(0, zz) if part == 2 else block(part, 0, 0, zz, c)
+        r_sem = meta_recv.at[0, zz] if part == 2 else recv_sem.at[part, 0, 0, zz]
+        for step in range(1, Z):
+            start(ref, line_send.at[part * Z + step], r_sem, (((z + step) % Z) * Y + y, v))
+
+    def second(zz):
+        arrived(0, 1, 0, zz)
+        along_x(0, 1, zz)
+        to_core(0, 1, 0, zz)
+        for dx in range(1, X):
+            arrived(1, 0, dx, zz)
+            along_y(1, dx, zz)
+            to_core(1, 0, dx, zz)
+
+    for t, zz in enumerate(order):
         for m in (0, 1):
-            send(m, (0, 0, 0), (0, 0, d), (((z + d) % Z) * Y + y, v))
-    for step in range(1, rows):
-        other = (r + step) % rows
-        copy = remote(
-            meta.at[own_meta], meta.at[own_meta], meta_send.at[step], meta_recv.at[step], (other, v)
-        )
-        copy.start()
-        sends.append(copy)
-
-    def along_y(m, ax, d):
-        send(m, (0, ax, d), (1, ax, d), (z * Y + 1 - y, v))
-
-    def along_x(m, ay, d):
-        for dx in range(1, X):
-            send(m, (ay, 0, d), (ay, dx, d), (r, ((x + dx) % X) * C + c))
-
-    for d in range(Z):
-        for m in (0, 1):
-            if d:
-                arrived(m, (0, 0, d))
+            if t:
+                arrived(m, 0, 0, zz)
+            pass_on(t, zz, m)
             if m == 0:
-                along_y(m, 0, d)
+                along_y(0, 0, zz)
             else:
-                along_x(m, 0, d)
-            to_core(m, (0, 0, d))
-    for d in range(Z):
-        along_x(0, 0, d)
-        along_y(1, 0, d)
-        arrived(0, (1, 0, d))
-        along_x(0, 1, d)
-        to_core(0, (1, 0, d))
-        for dx in range(1, X):
-            arrived(1, (0, dx, d))
-            along_y(1, dx, d)
-            to_core(1, (0, dx, d))
-    for d in range(Z):
+                along_x(1, 0, zz)
+                along_x(0, 0, zz)
+                along_y(1, 0, zz)
+        if t:
+            landed(meta_at(0, zz), meta_send.at[0, zz], meta_recv.at[0, zz])
+        pass_on(t, zz, 2)
+        start(meta_at(0, zz), meta_send.at[1, zz], meta_recv.at[1, zz], (z * Y + 1 - y, v))
+        to_core(0, 0, 0, zz)
+        to_core(1, 0, 0, zz)
+    for zz in order:
+        second(zz)
+    for zz in order:
         for dx in range(1, X):
             for ay in range(Y):
-                arrived(0, (ay, dx, d))
-                to_core(0, (ay, dx, d))
+                arrived(0, ay, dx, zz)
+                to_core(0, ay, dx, zz)
         for dx in range(X):
-            arrived(1, (1, dx, d))
-            to_core(1, (1, dx, d))
-
-    for step in range(1, rows):
-        src = (r + rows - step) % rows
-        slot = (src % Y) * Z + src // Y
-        remote(
-            meta.at[slot], meta.at[slot], meta_send.at[step], meta_recv.at[step], (r, v)
-        ).wait_recv()
+            arrived(1, 1, dx, zz)
+            to_core(1, 1, dx, zz)
+
+    for zz in order:
+        landed(meta_at(1, zz), meta_send.at[1, zz], meta_recv.at[1, zz])
     target_cols, pos_cols, flag_cols = [], [], []
     for q in range(rows):
         pack = (q % Z) * Y + q // Z
@@ -207,13 +231,14 @@
 
     stat_cols = []
     for m, gain in enumerate((gain_p, gain_r)):
-        for d in range(Z):
+        for zz in order:
             for ay in range(Y):
                 for ax in range(X):
-                    dst = block(m, ay, ax, d, 1 - c)
-                    remote(
-                        dst, dst, core_send.at[m, ay, ax, d], core_recv.at[m, ay, ax, d], (r, v)
-                    ).wait_recv()
+                    landed(
+                        block(m, ay, ax, zz, 1 - c),
+                        core_send.at[m, ay, ax, zz],
+                        core_recv.at[m, ay, ax, zz],
+                    )
         head_copies[m].wait()
         total = jnp.zeros((n_tok, 1), F32)
         for part in range(vocab):
@@ -223,7 +248,7 @@
         logits = jnp.zeros((n_tok, vcols), F32)
         for part in range(vocab):
             piece = gathered[m, part].reshape(n_tok, feat).astype(F32)
-            weight = gain[0:1, part * feat : (part + 1) * feat].astype(F32)
+            weight = gain[pl.ds(part * feat, feat)].astype(F32).reshape(1, feat)
             normed = (piece * inverse_rms * weight).astype(BF16)
             logits = logits + jnp.dot(
                 normed, heads[m, part * feat : (part + 1) * feat, :], preferred_element_type=F32
@@ -340,8 +365,9 @@
             dma((2, 2, x, z)),
             dma((2, 2, x, z)),
             dma((2, 2, x, z)),
-            dma((rows,)),
-            dma((rows,)),
+            dma((3 * (z + 1),)),
+            dma((2, z)),
+            dma((2, z)),
             dma((devices,)),
             dma((devices,)),
         ],
@@ -351,8 +377,8 @@
     )(
         hidden_policy,
         hidden_reference,
-        row(gain_policy),
-        row(gain_reference),
+        gain_policy,
+        gain_reference,
         head_policy,
         head_reference,
         row(targets),

time: 36.2 us -> 31.7 us (0.88)
  local copies, waits for them, and re-layouts: 4.88 us -> 2.25 us
  Pallas kernels: 30.4 us -> 28.7 us
    reshape x2 -> x0, local copies, waits for them, and re-layouts: 2.56 us -> none  [per_device(): row = lambda a: a.reshape(1, a.shape[0])]
    pallas_call x1, Pallas kernels: 30.4 us -> 28.7 us  [per_device(): pl.pallas_call(functools.partial(kernel, rows, vocab), out_shape=(jax.Sha...]
where the time goes in v2:
time: 31.7 us; the launch traced here: 31.6 us
  Pallas kernels  28.7 us (91%)
  local copies, waits for them, and re-layouts  2.25 us (7%)
  between operations  0.64 us (2%)
    pallas_call x1, Pallas kernels, per_device(): pl.pallas_call(functools.partial(kernel, rows, vocab), out_shape=(jax.Sha...  28.7 us
    squeeze x1, local copies, waits for them, and re-layouts, per_device(): return (lp.reshape(CAP), adv[0, :DOC_DEV])  1.14 us
    unnamed x1, local copies, waits for them, and re-layouts  1.11 us

profile of v2, /device:TPU:0, one launch (start us, length us, event | category | flops | bytes accessed | tf_op | source)
XLA Modules:
  0.0 31.6 jit_solution(18167130748129784287)
XLA Ops:
  0.6 28.7 %shard_map.122 = (f32[1,128]{1,0:T(1,128)}, f32[1,128]{1,0:T(1,128)}) custom-call(bf16[64,384]{1,0:T(8,128)(2,1)} %hidden_p.1, bf16[64,384]{1,0:T(8,128)(2,1)} %hidden_r.1, bf16[1536]{0:T(1024)(128)(2,1)} %gain_p.1, bf16[1536]{0:T(1024)(128)(2,1)} %gain_r.1, bf16[1536,512]{1,0:T(8,128)(2,1)} %head_p.1, bf16[1536,512]{1,0:T(8,128)(2,1)} %head_r.1, ...), custom_call_target="tpu_custom_call" | custom-call | tf_op jit(solution)/shard_map/pallas_call | solution.py:350
  29.3 1.1 %slice_bitcast_fusion = f32[2]{0:T(128)} fusion(f32[1,128]{1,0:T(1,128)} %get-tuple-element.5), kind=kLoop, calls=%fused_computation | loop fusion | bytes 16 | tf_op jit(solution)/shard_map/squeeze | solution.py:390
  30.4 1.1 %copy.14 = f32[128]{0:T(128)} copy(f32[128]{0:T(128)} %bitcast.13) | data formatting | bytes 1024

commit v3 on v2

--- a/solution.py
+++ b/solution.py
@@ -321,6 +321,11 @@
     out_lp[...] = col_to_row(jnp.sum(jnp.where(lands, lp_p, 0.0), axis=1, keepdims=True))
     for copy in sends:
         copy.wait_send()
+
+
+def write_out(lp, adv, out_lp, out_adv):
+    out_lp[...] = lp[0]
+    out_adv[...] = adv[0, 0:DOC_DEV]
 
 
 def per_device(
@@ -387,7 +392,12 @@
         row(doc_owner),
         row(doc_score),
     )
-    return lp.reshape(CAP), adv[0, :DOC_DEV]
+    return pl.pallas_call(
+        write_out,
+        out_shape=(jax.ShapeDtypeStruct((CAP,), F32), jax.ShapeDtypeStruct((DOC_DEV,), F32)),
+        in_specs=[vmem] * 2,
+        out_specs=(vmem, vmem),
+    )(lp, adv)
 
 
 def solution(mesh):

time: 31.7 us -> 30.6 us (0.965)
  local copies, waits for them, and re-layouts: 2.25 us -> 0 us
  Pallas kernels: 28.7 us -> 29.8 us
    pallas_call x0 -> x1, Pallas kernels: none -> 1.15 us  [per_device(): pl.pallas_call(write_out, out_shape=(jax.ShapeDtypeStruct((CAP,), F32), j...]
    squeeze x1 -> x0, local copies, waits for them, and re-layouts: 1.14 us -> none  [per_device(): return (lp.reshape(CAP), adv[0, :DOC_DEV])]
    unnamed x1 -> x0, local copies, waits for them, and re-layouts: 1.11 us -> none
where the time goes in v3:
time: 30.6 us; the launch traced here: 30.5 us
  Pallas kernels  29.8 us (97%)
  between operations  0.64 us (2%)
    pallas_call x1, Pallas kernels, per_device(): pl.pallas_call(functools.partial(kernel, rows, vocab), out_shape=(jax.Sha...  28.7 us
    pallas_call x1, Pallas kernels, per_device(): pl.pallas_call(write_out, out_shape=(jax.ShapeDtypeStruct((CAP,), F32), j...  1.15 us

profile of v3, /device:TPU:0, one launch (start us, length us, event | category | flops | bytes accessed | tf_op | source)
XLA Modules:
  0.0 30.5 jit_solution(14501132030747332039)
XLA Ops:
  0.6 28.7 %shard_map.122 = (f32[1,128]{1,0:T(1,128)}, f32[1,128]{1,0:T(1,128)}) custom-call(bf16[64,384]{1,0:T(8,128)(2,1)} %hidden_p.1, bf16[64,384]{1,0:T(8,128)(2,1)} %hidden_r.1, bf16[1536]{0:T(1024)(128)(2,1)} %gain_p.1, bf16[1536]{0:T(1024)(128)(2,1)} %gain_r.1, bf16[1536,512]{1,0:T(8,128)(2,1)} %head_p.1, bf16[1536,512]{1,0:T(8,128)(2,1)} %head_r.1, ...), custom_call_target="tpu_custom_call" | custom-call | tf_op jit(solution)/shard_map/pallas_call | solution.py:355
  29.3 1.1 %shard_map.123 = (f32[128]{0:T(128)}, f32[2]{0:T(128)}) custom-call(f32[1,128]{1,0:T(1,128)} %get-tuple-element.4.lp, f32[1,128]{1,0:T(1,128)} %get-tuple-element.5.adv), custom_call_target="tpu_custom_call" | custom-call | tf_op jit(solution)/shard_map/pallas_call | solution.py:395
